TPU v7x, 32 devices: a whole 2x2x4 slice. The times are simulated.
32 devices in a mesh: grp: 2 (over x), ctr: 16 (over z, y, core).
Axes of the slice: x: 2, y: 2, z: 4, core: 2. Of those that a mesh axis runs over, the one named last changes fastest.
Arguments:
- centres: bfloat16 [6144, 768], P(('grp', 'ctr')), parts along dimension 0
- sample_idx: int32 [1024], P(('grp', 'ctr')), parts along dimension 0, may hold values from 0 to 3071, as said below
- coef: float32 [6144], P(('grp', 'ctr')), parts along dimension 0
- metric_factor: bfloat16 [768, 768], replicated, may hold values from -0.21875 to 0.21875
Outputs:
- metric_new: float32 [1536, 768], P(('grp', 'ctr')), parts along dimension 0
- transformed: float32 [1024, 768], P(('grp', 'ctr')), parts along dimension 0
There are 2 independent parts, one for each index of `grp`. A program takes and returns all parts, laid end to end along the dimension named above; an argument that names none is the same for every part. Nothing has to cross between parts.
Inputs may be any that keep to these rules, and one draw needn't show every extreme that they name: The 32 samples of the k-th aligned block of sample_idx are distinct centres of the k-th block of 192 centres.
All inputs are finite; a program needn't handle non-finite values.
Results may differ from a plain program's by a relative error of at most 0.0031.
Values may be sent and summed in bfloat16 or wider, within the bound.
A program may use at most 128 MiB of HBM per device.

v0:
```python
import jax
import jax.numpy as jnp
from jax import lax
from jax.sharding import PartitionSpec as P


def block_grad(rows_u, v_own, sv_own, coef):
    width = rows_u.shape[1]
    su = jnp.sum(rows_u.astype(jnp.float32) ** 2, axis=1)
    cross = jnp.dot(rows_u, v_own.T, preferred_element_type=jnp.float32)
    dist_sq = jnp.maximum(su[:, None] + sv_own[None, :] - 2.0 * cross, 0.0)
    radius = jnp.sqrt(dist_sq / width + 1.0)
    weight = coef[None, :] * jnp.exp(-radius / 4.0) / (4.0 * width * radius)
    wround = weight.astype(jnp.bfloat16)
    return jnp.dot(wround, v_own, preferred_element_type=jnp.float32) - jnp.sum(weight, axis=1)[
        :, None
    ] * rows_u.astype(jnp.float32)


def local(centres, sample_idx, coef, metric_factor):
    width = centres.shape[1]
    own_count = sample_idx.shape[0]
    devices = lax.axis_size("ctr")
    offset = lax.axis_index("ctr") * centres.shape[0]
    own_rows = jnp.take(centres, sample_idx - offset, axis=0)
    u_own = jnp.dot(own_rows, metric_factor, preferred_element_type=jnp.float32).astype(
        jnp.bfloat16
    )
    v_own = jnp.dot(centres, metric_factor, preferred_element_type=jnp.float32).astype(jnp.bfloat16)
    factor = metric_factor.astype(jnp.float32)
    coef_full = lax.all_gather(coef, "ctr", axis=0, tiled=True)
    piece = lax.all_gather(v_own, "ctr", axis=0, tiled=True)
    sv_piece = jnp.sum(piece.astype(jnp.float32) ** 2, axis=1)
    summed = block_grad(u_own, piece, sv_piece, coef_full)
    grads = jnp.dot(summed, factor.T, precision=lax.Precision.HIGHEST)
    local_outer = jnp.dot(grads.T, grads, precision=lax.Precision.HIGHEST) / (own_count * devices)
    agop = lax.psum(local_outer, "ctr")
    metric_full = agop * width / jnp.trace(agop)
    row_count = width // devices
    metric_rows = lax.dynamic_slice_in_dim(
        metric_full, lax.axis_index("ctr") * row_count, row_count, 0
    )
    transformed = jnp.dot(grads, metric_full, precision=lax.Precision.HIGHEST)
    return (metric_rows, transformed)


def solution(mesh):
    placed = (P(("grp", "ctr"), None), P(("grp", "ctr")), P(("grp", "ctr")), P())
    return jax.shard_map(
        local,
        mesh=mesh,
        in_specs=placed,
        out_specs=(P(("grp", "ctr"), None), P(("grp", "ctr"), None)),
        check_vma=False,
    )
```

profile of v0, /device:TPU:0, one launch (start us, length us, event | category | flops | bytes accessed | tf_op | source)
XLA Modules:
  0.0 199.3 jit_solution(7842170020570275571)
XLA Ops:
  7.2 0.0 copy-start
  7.2 0.0 copy-start.4
  7.2 0.0 copy-start.3
  7.2 0.0 all-gather.2.cloned.1.call-start
  7.2 1.2 copy-done
  8.4 2.1 %convolution_convert_fusion = bf16[192,768]{1,0:T(8,128)(2,1)} fusion(bf16[192,768]{1,0:T(8,128)(2,1)} %param.4, bf16[768,768]{1,0:T(8,128)(2,1)S(1)} %copy-done), kind=kOutput, calls=%fused_computation.12 | convolution fusion | flops 226639872 | bytes 1769472 | tf_op jit(solution)/shard_map/dot_general | solution.py:29
  10.5 0.0 all-gather.2.cloned.1.call-update
  10.5 0.0 all-reduce.3.cloned.1.call-start
  10.6 0.7 compare_and_fusion
  11.3 1.7 gather_fusion
  12.9 0.0 copy-done.4
  12.9 0.6 dynamic-slice
  14.2 0.0 copy-done.3
  14.2 0.3 dynamic-update-slice
  14.5 64.2 %all-reduce = f32[3072]{0:T(1024)S(1)} all-reduce(f32[3072]{0:T(1024)S(1)} %dynamic-update-slice), channel_id=1, replica_groups=mesh['grp'=2,'ctr'=16] {'ctr'}, use_global_device_ids=true, to_apply=%add | all-reduce | flops 3072 | bytes 24576
  78.7 0.5 fusion.6
  79.1 0.0 all-gather.2.cloned.1.call-done
  79.2 0.0 copy-start.1
  79.2 3.5 %multiply_reduce_fusion = f32[3072]{0:T(1024)S(1)} fusion(bf16[3072,768]{1,0:T(8,128)(2,1)} %all-gather.2.cloned.1.call-done), kind=kLoop, calls=%fused_computation.1 | loop fusion | flops 7074816 | bytes 4730880 | tf_op jit(solution)/shard_map/reduce_sum | solution.py:33
  82.7 0.3 copy-done.1
  82.9 1.7 fusion.11
  84.6 0.9 convolution_subtract_fusion
  85.4 1.1 fusion.12
  86.6 3.5 %convolution_multiply_fusion.1 = f32[768,768]{1,0:T(8,128)} fusion(f32[32,768]{1,0:T(8,128)S(1)} %fusion.12), kind=kOutput, calls=%fused_computation.11 | convolution fusion | flops 227082240 | bytes 2457600 | tf_op jit(solution)/shard_map/dot_general | solution.py:36
  90.1 0.0 all-reduce.3.cloned.1.call-update
  90.1 96.2 %all-reduce.3.cloned.1.call-done = f32[768,768]{1,0:T(8,128)} async-done(((f32[768,768]{1,0:T(8,128)}), f32[768,768]{1,0:T(8,128)}) %all-reduce.3.cloned.1.call-update) | async-done | bytes 2359312 | tf_op jit(solution)/shard_map/psum | solution.py:37
  186.3 0.0 copy-start.2
  186.3 2.5 %select_reduce_fusion = f32[]{:T(128)} fusion(f32[768,768]{1,0:T(8,128)} %all-reduce.3.cloned.1.call-done), kind=kLoop, calls=%fused_computation.8 | loop fusion | flops 1769471 | bytes 2359300 | tf_op jit(solution)/shard_map/jit(trace)/reduce_sum | solution.py:38
  188.8 0.0 copy-done.2
  188.8 0.8 multiply_divide_fusion
  189.7 2.1 %fusion.13 = f32[32,768]{1,0:T(8,128)} fusion(f32[32,768]{1,0:T(8,128)S(1)} %fusion.12, f32[768,768]{1,0:T(8,128)S(1)} %multiply_divide_fusion), kind=kOutput, calls=%fused_computation.30 | convolution fusion | flops 226492416 | bytes 2555904 | tf_op jit(solution)/shard_map/dot_general | solution.py:43
  191.7 0.7 constant_dynamic-slice_fusion
  (2 shorter events, 0.0 us)
Async XLA Ops:
  7.2 1.3 copy-start
  7.2 5.8 %copy-start.4 = (u32[32]{0:T(128)S(1)}, u32[32]{0:T(128)}, u32[]{:S(2)}) copy-start(u32[32]{0:T(128)} %constant.52) | copy-start | bytes 388
  7.2 7.0 %copy-start.3 = (f32[192]{0:T(256)S(1)}, f32[192]{0:T(256)}, u32[]{:S(2)}) copy-start(f32[192]{0:T(256)} %param.6) | copy-start | bytes 2308
  7.2 72.0 %all-gather.2.cloned.1.call-start = ((), (), s32[]{:S(2)}) async-start(), calls=%async_computation | async-start | bytes 5013504 | tf_op jit(solution)/shard_map/all_gather | solution.py:32
  10.5 175.8 %all-reduce.3.cloned.1.call-start = ((), (), s32[]{:S(2)}) async-start(), calls=%async_computation.1 | async-start | bytes 4718592 | tf_op jit(solution)/shard_map/psum | solution.py:37
  79.2 3.8 %copy-start.1 = (bf16[3072,768]{1,0:T(8,128)(2,1)S(1)}, bf16[3072,768]{1,0:T(8,128)(2,1)}, u32[]{:S(2)}) copy-start(bf16[3072,768]{1,0:T(8,128)(2,1)} %all-gather.2.cloned.1.call-done) | copy-start | bytes 14155780
  186.3 2.5 %copy-start.2 = (f32[768,768]{1,0:T(8,128)S(1)}, f32[768,768]{1,0:T(8,128)}, u32[]{:S(2)}) copy-start(f32[768,768]{1,0:T(8,128)} %all-reduce.3.cloned.1.call-done) | copy-start | bytes 7077892
Sparse Core Ops, SparseCore 0:
  10.7 56.3 all-gather.1
  90.2 96.0 all-reduce.2
where the time goes:
time: 200 us; the launch traced here: 199 us
  waiting for transfers between devices  96.3 us (48%)
  blocking collectives  64.2 us (32%)
  between operations  14.8 us (7%)
  matrix products  11.8 us (6%)
  other arithmetic  7.48 us (4%)
  local copies, waits for them, and re-layouts  4.68 us (2%)
    psum x1, waiting for transfers between devices, local(): agop = lax.psum(local_outer, 'ctr')  96.2 us
    unnamed x1, blocking collectives  64.2 us
  transfers between devices with their start and end apart: 2, of which 1 were waited for; matrix products, arithmetic and copies ran while one was open for 2% of the time, Pallas kernels for 0%

commit v1 on v0

--- a/solution.py
+++ b/solution.py
@@ -34,7 +34,8 @@
     summed = block_grad(u_own, piece, sv_piece, coef_full)
     grads = jnp.dot(summed, factor.T, precision=lax.Precision.HIGHEST)
     local_outer = jnp.dot(grads.T, grads, precision=lax.Precision.HIGHEST) / (own_count * devices)
-    agop = lax.psum(local_outer, "ctr")
+    ready = lax.all_gather(local_outer, "ctr")
+    agop = jnp.sum(ready, axis=0)
     metric_full = agop * width / jnp.trace(agop)
     row_count = width // devices
     metric_rows = lax.dynamic_slice_in_dim(

time: 200 us -> 300 us (1.50)
  waiting for transfers between devices: 96.3 us -> 185 us
  other arithmetic: 7.48 us -> 19.4 us
    all_gather x0 -> x1, waiting for transfers between devices: none -> 185 us  [local(): ready = lax.all_gather(local_outer, 'ctr')]
    psum x1 -> x0, waiting for transfers between devices: 96.2 us -> none  [local(): agop = lax.psum(local_outer, 'ctr')]
    reduce_sum x0 -> x1, other arithmetic: none -> 13.7 us  [local(): agop = jnp.sum(ready, axis=0)]
  transfers between devices with their start and end apart: 2 -> 2, of which waited for: 1 -> 1; matrix products, arithmetic and copies ran while one was open for 2% -> 1% of each run, Pallas kernels for 0% -> 0%
where the time goes in v1:
time: 300 us
  waiting for transfers between devices  185 us (62%)
  blocking collectives  64.6 us (22%)
  other arithmetic  19.4 us (6%)
  between operations  14.8 us (5%)
  matrix products  11.8 us (4%)
  local copies, waits for them, and re-layouts  4.45 us (1%)
    all_gather x1, waiting for transfers between devices, local(): ready = lax.all_gather(local_outer, 'ctr')  185 us
    unnamed x1, blocking collectives  64.6 us
    reduce_sum x1, other arithmetic, local(): agop = jnp.sum(ready, axis=0)  13.7 us
  transfers between devices with their start and end apart: 2, of which 1 were waited for; matrix products, arithmetic and copies ran while one was open for 1% of the time, Pallas kernels for 0%

profile of v1, /device:TPU:0, one launch (start us, length us, event | category | flops | bytes accessed | tf_op | source)
XLA Modules:
  0.0 300.0 jit_solution(10525340048923902765)
XLA Ops:
  7.2 0.0 copy-start
  7.2 0.0 copy-start.6
  7.2 0.0 copy-start.2
  7.2 0.0 copy-start.5
  7.2 0.0 all-gather.4.cloned.1.call-start
  7.3 1.3 copy-done
  8.5 2.1 convolution_convert_fusion
  10.6 0.0 all-gather.4.cloned.1.call-update
  10.6 0.0 all-gather.6.cloned.1.call-start
  10.7 0.7 compare_and_fusion
  11.4 0.0 copy-done.2
  11.4 0.6 gather_fusion
  12.0 0.0 copy-done.6
  12.0 0.6 dynamic-slice
  13.3 0.0 copy-done.5
  13.3 0.3 dynamic-update-slice
  13.6 64.6 %all-reduce = f32[3072]{0:T(1024)S(1)} all-reduce(f32[3072]{0:T(1024)S(1)} %dynamic-update-slice), channel_id=1, replica_groups=mesh['grp'=2,'ctr'=16] {'ctr'}, use_global_device_ids=true, to_apply=%add | all-reduce | flops 3072 | bytes 24576
  78.1 0.5 fusion.6
  78.6 0.0 all-gather.4.cloned.1.call-done
  78.6 0.0 copy-start.1
  78.6 3.5 %multiply_reduce_fusion = f32[3072]{0:T(1024)S(1)} fusion(bf16[3072,768]{1,0:T(8,128)(2,1)} %all-gather.4.cloned.1.call-done), kind=kLoop, calls=%fused_computation.1 | loop fusion | flops 7074816 | bytes 4730880 | tf_op jit(solution)/shard_map/reduce_sum | solution.py:33
  82.1 0.3 copy-done.1
  82.4 1.6 fusion.11
  84.0 0.9 convolution_subtract_fusion
  84.9 1.1 fusion.12
  86.0 0.0 copy-start.3
  86.0 0.7 copy-done.3
  86.7 3.5 %convolution_multiply_fusion.1 = f32[768,768]{1,0:T(8,128)} fusion(f32[32,768]{1,0:T(8,128)S(1)} %fusion.12), kind=kOutput, calls=%fused_computation.11 | convolution fusion | flops 227082240 | bytes 2457600 | tf_op jit(solution)/shard_map/dot_general | solution.py:36
  90.2 0.0 all-gather.6.cloned.1.call-update
  90.2 184.9 %all-gather.6.cloned.1.call-done = f32[12288,768]{1,0:T(8,128)} async-done(((f32[768,768]{1,0:T(8,128)}), f32[12288,768]{1,0:T(8,128)}) %all-gather.6.cloned.1.call-update) | async-done | bytes 37748752 | tf_op jit(solution)/shard_map/all_gather | solution.py:37
  275.1 13.7 %reduce_sum.49 = f32[768,768]{1,0:T(8,128)S(1)} reduce(f32[16,768,768]{2,1,0:T(8,128)} %bitcast.15, f32[]{:T(128)} %constant.20.clone.1), dimensions={0}, to_apply=%region_3.4 | reduce | flops 8847360 | bytes 40108036 | tf_op jit(solution)/shard_map/reduce_sum | solution.py:38
  288.8 0.7 select_reduce_fusion
  289.5 0.0 copy-start.4
  289.5 0.8 multiply_divide_fusion
  290.3 0.1 copy-done.4
  290.4 2.1 fusion.13
  292.5 0.7 constant_dynamic-slice_fusion
  (2 shorter events, 0.0 us)
Async XLA Ops:
  7.2 1.4 copy-start
  7.2 4.8 %copy-start.6 = (u32[32]{0:T(128)S(1)}, u32[32]{0:T(128)}, u32[]{:S(2)}) copy-start(u32[32]{0:T(128)} %constant.52) | copy-start | bytes 388
  7.2 4.2 %copy-start.2 = (bf16[192,768]{1,0:T(8,128)(2,1)S(1)}, bf16[192,768]{1,0:T(8,128)(2,1)}, u32[]{:S(2)}) copy-start(bf16[192,768]{1,0:T(8,128)(2,1)} %param.4) | copy-start | bytes 884740
  7.2 6.1 %copy-start.5 = (f32[192]{0:T(256)S(1)}, f32[192]{0:T(256)}, u32[]{:S(2)}) copy-start(f32[192]{0:T(256)} %param.6) | copy-start | bytes 2308
  7.2 71.4 %all-gather.4.cloned.1.call-start = ((), (), s32[]{:S(2)}) async-start(), calls=%async_computation | async-start | bytes 5013504 | tf_op jit(solution)/shard_map/all_gather | solution.py:32
  10.6 264.4 %all-gather.6.cloned.1.call-start = ((), (), s32[]{:S(2)}) async-start(), calls=%async_computation.1 | async-start | bytes 40108032 | tf_op jit(solution)/shard_map/all_gather | solution.py:37
  78.6 3.8 %copy-start.1 = (bf16[3072,768]{1,0:T(8,128)(2,1)S(1)}, bf16[3072,768]{1,0:T(8,128)(2,1)}, u32[]{:S(2)}) copy-start(bf16[3072,768]{1,0:T(8,128)(2,1)} %all-gather.4.cloned.1.call-done) | copy-start | bytes 14155780
  86.0 0.7 copy-start.3
  289.5 0.9 copy-start.4
Sparse Core Ops, SparseCore 0:
  10.7 56.1 all-gather.3
  90.3 184.7 all-gather.5
